TPU v7x, 32 devices: a whole 2x2x4 slice. The times are simulated.
32 devices in a mesh: row: 8 (over y, x, core), ctx: 4 (over z).
Axes of the slice: x: 2, y: 2, z: 4, core: 2. Of those that a mesh axis runs over, the one named last changes fastest.
Arguments:
- queries: bfloat16 [5, 4096, 128], P(None, ('row', 'ctx')), may hold values from -100 to 100
- keys: bfloat16 [4096, 128], P('ctx'), may hold values from -6 to 6
- doc_ids: int32 [64], replicated, may hold values from 0 to 3, never falling along the last dimension, each value on 1 to 48 neighbouring positions
- gate_query: bfloat16 [5, 128, 128], replicated, may hold values from -0.5 to 0.5
- gate_key: bfloat16 [384, 128], replicated, may hold values from -0.3125 to 0.3125
Outputs:
- block_map: float32 [5, 64, 64], P(None, ('row', 'ctx'))
- grad_query: float32 [5, 128, 128], replicated
- grad_key: float32 [384, 128], replicated
Inputs may be any that keep to these rules, and one draw needn't show every extreme that they name: `doc_ids`: block document ids never fall along the sequence; each document spans 1 to 48 blocks and one spans exactly 48.
All inputs are finite; a program needn't handle non-finite values.
Results may differ from a plain program's by a relative error of at most 0.0003.
Values may be sent and summed in bfloat16 or wider, within the bound.
A program may use at most 64 MiB of HBM per device.

v0:
```python
import math

import jax
import jax.numpy as jnp
from jax import lax
from jax.sharding import PartitionSpec as P

BLK = 64


NEG_FILL = -1e30
BLOCK_CAP = 512


def pool_keys(key_block, block_len):
    grouped = key_block.astype(jnp.float32).reshape(
        key_block.shape[0] // block_len, block_len, key_block.shape[1]
    )
    return jnp.concatenate(
        [jnp.max(grouped, axis=1), jnp.min(grouped, axis=1), jnp.mean(grouped, axis=1)], axis=1
    )


def held_positions(row_index, ctx_index, ctx_total, row_count):
    half_rows = row_count // 2
    home_start = (row_index * ctx_total + ctx_index) * row_count
    far_start = home_start + half_rows
    offsets = jnp.arange(half_rows, dtype=jnp.int32)
    return jnp.concatenate([home_start + offsets, far_start + offsets])


def block_docs(doc_ids, positions, block_len):
    block_starts = positions.reshape(-1, block_len)[:, 0] // block_len
    return jnp.repeat(jnp.take(doc_ids, block_starts), block_len)


def tile_update(
    carried,
    held_rows,
    query_pos,
    query_doc,
    key_block,
    key_start,
    table_base,
    doc_ids,
    block_len,
    score_scale,
):
    score_table, row_max, row_sum = carried
    key_count = key_block.shape[0]
    head_count, row_count = (held_rows.shape[0], held_rows.shape[1])
    scores = (
        jnp.einsum("hrd,kd->hrk", held_rows, key_block, preferred_element_type=jnp.float32)
        * score_scale
    )
    key_pos = key_start + jnp.arange(key_count, dtype=jnp.int32)
    key_doc = jnp.repeat(
        lax.dynamic_slice_in_dim(doc_ids, key_start // block_len, key_count // block_len), block_len
    )
    allowed = (key_pos[None, :] <= query_pos[:, None]) & (key_doc[None, :] == query_doc[:, None])
    masked = jnp.where(allowed[None], scores, NEG_FILL)
    block_peaks = jnp.max(
        masked.reshape(head_count, row_count, key_count // block_len, block_len), axis=3
    )
    score_table = lax.dynamic_update_slice_in_dim(
        score_table, block_peaks, (key_start - table_base) // block_len, 2
    )
    new_max = jnp.maximum(row_max, jnp.max(masked, axis=2))
    weights = jnp.where(allowed[None], jnp.exp(masked - new_max[:, :, None]), 0.0)
    row_sum = row_sum * jnp.exp(row_max - new_max) + jnp.sum(weights, axis=2)
    return (score_table, new_max, row_sum)


def finish_maps(score_table, row_max, row_sum, block_len):
    log_total = row_max + jnp.log(row_sum)
    chances = jnp.exp(score_table - log_total[:, :, None])
    head_count, row_count, column_count = chances.shape
    return jnp.max(
        chances.reshape(head_count, row_count // block_len, block_len, column_count), axis=2
    )


def key_pass(
    held_rows, query_pos, query_doc, key_shard, doc_ids, block_len, score_scale, total_blocks
):
    head_count, row_count, head_dim = held_rows.shape
    query_top = jnp.max(query_pos)
    doc_floor = jnp.min(query_doc)
    initial = (
        jnp.full((head_count, row_count, total_blocks), NEG_FILL, jnp.float32),
        jnp.full((head_count, row_count), NEG_FILL, jnp.float32),
        jnp.zeros((head_count, row_count), jnp.float32),
        jnp.zeros((total_blocks, 3 * head_dim), jnp.float32),
    )
    key_piece = lax.all_gather(key_shard, "ctx", axis=0, tiled=True)
    piece_rows = key_piece.shape[0]
    sub_rows = math.gcd(piece_rows, BLOCK_CAP)

    def advance(turn_index, inner):
        stats = inner[:3]
        pooled = inner[3]
        key_start = turn_index * sub_rows
        key_block = lax.dynamic_slice_in_dim(key_piece, turn_index * sub_rows, sub_rows, 0)
        pooled = lax.dynamic_update_slice_in_dim(
            pooled, pool_keys(key_block, block_len), key_start // block_len, 0
        )

        def sweep(current):
            return tile_update(
                current,
                held_rows,
                query_pos,
                query_doc,
                key_block,
                key_start,
                0,
                doc_ids,
                block_len,
                score_scale,
            )

        def keep_stats(current):
            return current

        last_doc = lax.dynamic_index_in_dim(
            doc_ids, (key_start + sub_rows - 1) // block_len, 0, keepdims=False
        )
        needed = (key_start <= query_top) & (last_doc >= doc_floor)
        stats = lax.cond(needed, sweep, keep_stats, stats)
        return stats + (pooled,)

    score_table, row_max, row_sum, pooled = lax.fori_loop(
        0, piece_rows // sub_rows, advance, initial
    )
    return (finish_maps(score_table, row_max, row_sum, block_len), pooled)


def gate_gradients(query_pool, pooled, gate_query, gate_key, block_map, block_allowed):
    query_gate = jnp.einsum(
        "hbd,hde->hbe", query_pool, gate_query.astype(jnp.float32), precision=lax.Precision.HIGHEST
    )
    key_gate = jnp.dot(pooled, gate_key.astype(jnp.float32), precision=lax.Precision.HIGHEST)
    gate_logits = jnp.einsum("hbe,ke->hbk", query_gate, key_gate, precision=lax.Precision.HIGHEST)
    gate_exp = jnp.where(block_allowed[None], jnp.exp(gate_logits), 0.0)
    gate_prob = gate_exp / jnp.sum(gate_exp, axis=2, keepdims=True)
    target = block_map / jnp.sum(block_map, axis=2, keepdims=True)
    diff = gate_prob - target
    query_back = jnp.einsum("hbk,ke->hbe", diff, key_gate, precision=lax.Precision.HIGHEST)
    query_term = jnp.einsum("hbd,hbe->hde", query_pool, query_back, precision=lax.Precision.HIGHEST)
    key_back = jnp.einsum("hbk,hbe->ke", diff, query_gate, precision=lax.Precision.HIGHEST)
    key_term = jnp.dot(pooled.T, key_back, precision=lax.Precision.HIGHEST)
    return (query_term, key_term)


def shards(queries, keys, doc_ids, gate_query, gate_key):
    head_count, row_count, head_dim = queries.shape
    block_len = BLK
    total_blocks = doc_ids.shape[0]
    score_scale = 1.0 / math.sqrt(head_dim)
    ctx_total = lax.axis_size("ctx")
    row_index = lax.axis_index("row")
    ctx_index = lax.axis_index("ctx")
    query_pos = held_positions(row_index, ctx_index, ctx_total, row_count)
    query_doc = block_docs(doc_ids, query_pos, block_len)
    held_maps, pooled = key_pass(
        queries, query_pos, query_doc, keys, doc_ids, block_len, score_scale, total_blocks
    )
    home_count = row_count // block_len
    home_blocks = (row_index * ctx_total + ctx_index) * home_count + jnp.arange(
        home_count, dtype=jnp.int32
    )
    home_docs = jnp.take(doc_ids, home_blocks)
    all_blocks = jnp.arange(total_blocks, dtype=jnp.int32)
    block_allowed = (all_blocks[None, :] <= home_blocks[:, None]) & (
        doc_ids[None, :] == home_docs[:, None]
    )
    query_pool = jnp.mean(
        queries.astype(jnp.float32).reshape(head_count, home_count, block_len, head_dim), axis=2
    )
    query_term, key_term = gate_gradients(
        query_pool, pooled, gate_query, gate_key, held_maps, block_allowed
    )
    grad_query, grad_key = lax.psum((query_term, key_term), ("row", "ctx"))
    return (held_maps, grad_query, grad_key)


def solution(mesh):
    in_specs = (P(None, ("row", "ctx"), None), P("ctx", None), P(), P(), P())
    out_specs = (P(None, ("row", "ctx"), None), P(), P())
    return jax.shard_map(shards, mesh=mesh, in_specs=in_specs, out_specs=out_specs, check_vma=False)
```

profile of v0, /device:TPU:0, one launch (start us, length us, event | category | flops | bytes accessed | tf_op | source)
XLA Modules:
  0.0 223.4 jit_solution(13385890775669702233)
XLA Ops:
  7.2 0.7 all-gather.2.cloned.1.call-update
  8.3 1.3 gather_fusion
  9.6 1.3 gather_fusion.1
  10.9 0.6 fusion.18
  12.9 0.7 broadcast_reduce_fusion
  14.0 26.4 %all-gather.2.cloned.1.call-done = bf16[4096,128]{1,0:T(8,128)(2,1)} async-done(((bf16[1024,128]{1,0:T(8,128)(2,1)}), bf16[4096,128]{1,0:T(8,128)(2,1)}) %all-gather.2.cloned.1.call-update) | async-done | bytes 1048592 | tf_op jit(solution)/shard_map/all_gather | solution.py:95
  40.4 27.2 %while.25 = (s32[]{:T(128)}, f32[5,128,64]{1,2,0:T(8,128)S(1)}, f32[5,128]{1,0:T(8,128)S(1)}, f32[5,128]{1,0:T(8,128)S(1)}, f32[64,384]{1,0:T(8,128)S(1)}, /*ind...) while((s32[]{:T(128)}, f32[5,128,64]{1,2,0:T(8,128)S(1)}, ...), condition=%wide.region_12.14_spmd.clone, body=%wide.region_3.13_spmd.clone.sunk | while | flops 86640432 | bytes 7622712 | solution.py:132
  40.4 1.0 bitcast_reduce_fusion.4
  41.7 0.6 dynamic_slice.37
  43.6 2.2 conditional.3
  44.1 0.4 fusion.23
  44.6 0.4 select_reduce_fusion
  45.0 0.4 copy.26
  45.8 0.9 bitcast_reduce_fusion.4
  47.0 0.6 dynamic_slice.37
  48.9 0.9 bitcast_reduce_fusion.4
  50.2 0.6 dynamic_slice.37
  52.0 0.9 bitcast_reduce_fusion.4
  53.3 0.6 dynamic_slice.37
  55.1 0.9 bitcast_reduce_fusion.4
  56.4 0.6 dynamic_slice.37
  58.3 0.9 bitcast_reduce_fusion.4
  59.5 0.6 dynamic_slice.37
  61.4 0.9 bitcast_reduce_fusion.4
  62.7 0.6 dynamic_slice.37
  64.5 0.9 bitcast_reduce_fusion.4
  65.8 0.6 dynamic_slice.37
  69.2 1.2 fusion.24
  70.4 1.4 fusion.8
  71.8 141.4 %all-reduce.3.cloned.1.call-done = (f32[5,128,128]{2,1,0:T(8,128)}, f32[384,128]{1,0:T(8,128)}) async-done(((f32[5,128,128]{2,1,0:T(8,128)}, f32[384,128]{1,0:T(8,128)}), (f32[5,128,128]{2,1,0:T(8,128)}, f32[384,128]{1,0:T(8,128)})) %all-reduce.3.cloned.1.call-update) | async-done | bytes 524304 | tf_op jit(solution)/shard_map/psum | solution.py:183
  213.2 1.7 copy.70
  214.9 1.6 copy.71
  (100 shorter events, 5.1 us)
Async XLA Ops:
  7.2 6.6 %copy-start = (bf16[5,128,128]{2,1,0:T(8,128)(2,1)S(1)}, bf16[5,128,128]{2,1,0:T(8,128)(2,1)}, u32[]{:S(2)}) copy-start(bf16[5,128,128]{2,1,0:T(8,128)(2,1)} %param.14) | copy-start | bytes 491524
  7.2 6.5 %copy-start.1 = (s32[64]{0:T(128)S(1)}, s32[64]{0:T(128)}, u32[]{:S(2)}) copy-start(s32[64]{0:T(128)} %param.13) | copy-start | bytes 772
  7.2 6.4 %copy-start.2 = (bf16[5,128,128]{2,1,0:T(8,128)(2,1)S(1)}, bf16[5,128,128]{2,1,0:T(8,128)(2,1)}, u32[]{:S(2)}) copy-start(bf16[5,128,128]{2,1,0:T(8,128)(2,1)} %param.11) | copy-start | bytes 491524
  7.2 33.2 %all-gather.2.cloned.1.call-start = ((), (), s32[]{:S(2)}) async-start(), calls=%async_computation | async-start | bytes 1310720 | tf_op jit(solution)/shard_map/all_gather | solution.py:95
  7.9 205.3 %all-reduce.3.cloned.1.call-start = ((), (), s32[]{:S(2)}) async-start(), calls=%async_computation.1 | async-start | bytes 1048576 | tf_op jit(solution)/shard_map/psum | solution.py:183
  40.4 27.7 %copy-start.3 = (bf16[384,128]{1,0:T(8,128)(2,1)S(1)}, bf16[384,128]{1,0:T(8,128)(2,1)}, u32[]{:S(2)}) copy-start(bf16[384,128]{1,0:T(8,128)(2,1)} %param.15) | copy-start | bytes 294916
  67.9 148.7 %copy-start.4 = (f32[5,2,64]{2,1,0:T(2,128)}, f32[5,2,64]{2,1,0:T(2,128)S(1)}, u32[]{:S(2)}) copy-start(f32[5,2,64]{2,1,0:T(2,128)S(1)} %bitcast_reduce_fusion.2) | copy-start | bytes 7684
Sparse Core Ops, SparseCore 0:
  9.6 30.7 all-gather.1
  71.9 141.2 all-reduce.2
where the time goes:
time: 222 us; the launch traced here: 223 us
  waiting for transfers between devices  168 us (76%)
  between operations  15.5 us (7%)
  local copies, waits for them, and re-layouts  13.4 us (6%)
  loops' own time  11 us (5%)
  other arithmetic  10.7 us (5%)
  matrix products  4.21 us (2%)
    psum x1, waiting for transfers between devices, shards(): grad_query, grad_key = lax.psum((query_term, key_term), ('row', 'ctx'))  141 us
    all_gather x1, waiting for transfers between devices, key_pass(): key_piece = lax.all_gather(key_shard, 'ctx', axis=0, tiled=True)  26.4 us
    another operation x1, loops' own time, key_pass(): lax.fori_loop(0, piece_rows // sub_rows, advance, initial)  10.8 us
    reduce_max x16, other arithmetic, pool_keys(): jnp.max(grouped, axis=1)  7.65 us
    dynamic_slice x8, local copies, waits for them, and re-layouts, advance(): lax.dynamic_index_in_dim(doc_ids, (key_start + sub_rows - 1) // block_len...  4.69 us
  transfers between devices with their start and end apart: 2, of which 2 were waited for; matrix products, arithmetic and copies ran while one was open for 2% of the time, Pallas kernels for 0%

commit v1 on v0

v1 whole, which is shorter than its diff:
```python
import functools
import math

import jax
import jax.numpy as jnp
from jax import lax
from jax.experimental import pallas as pl
from jax.experimental.pallas import tpu as pltpu
from jax.sharding import PartitionSpec as P

BLK = 64
NEG = -1e30
PIECE = 16
LANES = 128
MESH = pl.DeviceIdType.MESH
HI = lax.Precision.HIGHEST


def fdot(a, b, dims):
    return lax.dot_general(a, b, (dims, ((), ())), precision=HI, preferred_element_type=jnp.float32)


def kernel(
    R, C, q_ref, k_ref, doc_ref, gq_ref, gk_ref,
    bm_ref, dq_ref, dk_ref,
    kbuf, q_t, peak, bsum, kpool, qp_own, diff_own, qp_all, diff_all,
    s1, s2, s3, rsem, small_send, small_recv,
):
    H, rows, D = q_ref.shape
    shard = k_ref.shape[0]
    nb = rows // BLK
    n = R * C
    TB = n * nb
    r = lax.axis_index("row")
    c = lax.axis_index("ctx")
    me = r * C + c
    core = lax.rem(r, 2)
    half = R // 2
    scale = 1.0 / math.sqrt(D)

    def ctx_peer(d):
        return lax.rem(c + d, C)

    def row_peer(d):
        return lax.rem(r + 2 * d, R)

    partner = r + 1 - 2 * core

    barrier = pltpu.get_barrier_semaphore()
    for d in range(1, C):
        pl.semaphore_signal(barrier, inc=1, device_id=(r, ctx_peer(d)), device_id_type=MESH)
    for d in range(1, half):
        pl.semaphore_signal(barrier, inc=1, device_id=(row_peer(d), c), device_id_type=MESH)
    pl.semaphore_signal(barrier, inc=1, device_id=(partner, c), device_id_type=MESH)

    qp_own[...] = jnp.zeros_like(qp_own)
    for h in range(H):
        qf = q_ref[h].astype(jnp.float32)
        q_t[:, h * rows:(h + 1) * rows] = qf.T.astype(jnp.bfloat16)
        for j in range(nb):
            qp_own[0, h * nb + j:h * nb + j + 1, :] = jnp.mean(
                qf[j * BLK:(j + 1) * BLK], axis=0, keepdims=True
            )
    peak[...] = jnp.full_like(peak, NEG)
    bsum[...] = jnp.zeros_like(bsum)
    if kpool.shape[1] > TB:
        kpool[...] = jnp.zeros_like(kpool)

    pl.semaphore_wait(barrier, C - 1 + half)

    def slot(cc, rr):
        return pl.ds(pl.multiple_of(cc * shard + rr * rows, rows), rows)

    def copy1(d):
        return pltpu.make_async_remote_copy(
            src_ref=k_ref.at[pl.ds(pl.multiple_of(r * rows, rows), rows)],
            dst_ref=kbuf.at[slot(c, r)],
            send_sem=s1.at[d], recv_sem=rsem.at[c * R + r],
            device_id=(r, ctx_peer(d)), device_id_type=MESH,
        )

    def copy2(d, e):
        cc = ctx_peer(d)
        return pltpu.make_async_remote_copy(
            src_ref=kbuf.at[slot(cc, r)], dst_ref=kbuf.at[slot(cc, r)],
            send_sem=s2.at[d * half + e], recv_sem=rsem.at[cc * R + r],
            device_id=(row_peer(e), c), device_id_type=MESH,
        )

    def copy3(d, e):
        cc, rr = ctx_peer(d), row_peer(e)
        return pltpu.make_async_remote_copy(
            src_ref=kbuf.at[slot(cc, rr)], dst_ref=kbuf.at[slot(cc, rr)],
            send_sem=s3.at[d * half + e], recv_sem=rsem.at[cc * R + rr],
            device_id=(partner, c), device_id_type=MESH,
        )

    def arrived(cc, rr):
        pltpu.make_async_copy(
            kbuf.at[slot(cc, rr)], kbuf.at[slot(cc, rr)], rsem.at[cc * R + rr]
        ).wait()

    for d in range(1, C):
        copy1(d).start()

    a0 = me * nb
    lane = lax.broadcasted_iota(jnp.int32, (1, rows), 1)
    qdoc = jnp.zeros((1, rows), jnp.int32)
    for j in range(nb):
        qdoc = jnp.where(lane // BLK == j, doc_ref[a0 + j], qdoc)

    def score(num, keys, diagonal):
        for h in range(H):
            s = jnp.dot(
                keys, q_t[:, h * rows:(h + 1) * rows], preferred_element_type=jnp.float32
            ) * scale
            if diagonal:
                ki = lax.broadcasted_iota(jnp.int32, (rows, rows), 0)
                qi = lax.broadcasted_iota(jnp.int32, (rows, rows), 1)
                s = jnp.where(ki <= qi, s, NEG)
            for j in range(nb):
                b = num * nb + j
                t = s[j * BLK:(j + 1) * BLK]
                top = jnp.max(t, axis=0, keepdims=True)
                total = jnp.sum(jnp.exp(t - top), axis=0, keepdims=True)
                peak[h, pl.ds(b, 1), :] = jnp.where(
                    qdoc == doc_ref[b], top, NEG
                )
                bsum[h, pl.ds(b, 1), :] = total

    def process(cc, rr):
        num = cc * R + rr
        keys = kbuf[slot(cc, rr), :]
        wide = keys.astype(jnp.float32)
        for j in range(nb):
            t = wide[j * BLK:(j + 1) * BLK]
            b = num * nb + j
            kpool[0, pl.ds(b, 1), :] = jnp.max(t, axis=0, keepdims=True)
            kpool[1, pl.ds(b, 1), :] = jnp.min(t, axis=0, keepdims=True)
            kpool[2, pl.ds(b, 1), :] = jnp.mean(t, axis=0, keepdims=True)

        @pl.when(num < me)
        def _():
            score(num, keys, False)

        @pl.when(num == me)
        def _():
            score(num, keys, True)

    kbuf[pl.ds(pl.multiple_of(c * shard, shard), shard), :] = k_ref[...]

    @pl.loop(0, R)
    def _(i):
        process(c, i)

    @pl.loop(1, C)
    def _(d):
        arrived(ctx_peer(d), r)
        for e in range(1, half):
            copy2(d, e).start()
        copy3(d, 0).start()

    @pl.loop(1, C)
    def _(d):
        process(ctx_peer(d), r)

    @pl.loop(1, C)
    def _(d):
        @pl.loop(1, half)
        def _(e):
            arrived(ctx_peer(d), row_peer(e))
            copy3(d, e).start()

    @pl.loop(0, (C - 1) * (half - 1))
    def _(i):
        process(ctx_peer(i // (half - 1) + 1), row_peer(i % (half - 1) + 1))

    other = partner

    @pl.loop(0, (C - 1) * half)
    def _(i):
        arrived(ctx_peer(i // half + 1), lax.rem(other + 2 * (i % half), R))

    def small(k, own, everyone, p):
        to = lax.rem(me + p, n)
        return pltpu.make_async_remote_copy(
            src_ref=own,
            dst_ref=everyone.at[:, pl.ds(pl.multiple_of(me * PIECE, PIECE), PIECE)],
            send_sem=small_send.at[k], recv_sem=small_recv.at[k],
            device_id=(to // C, to % C), device_id_type=MESH,
        )

    def small_wait(k, everyone):
        part = everyone.at[:, pl.ds(0, (n - 1) * PIECE)]
        pltpu.make_async_copy(part, part, small_recv.at[k]).wait()

    def small_sent(k, everyone):
        part = everyone.at[:, pl.ds(0, (n - 1) * PIECE)]
        pltpu.make_async_copy(part, part, small_send.at[k]).wait()

    @pl.loop(1, n)
    def _(p):
        small(0, qp_own, qp_all, p).start()

    @pl.loop(0, (C - 1) * half)
    def _(i):
        process(ctx_peer(i // half + 1), lax.rem(other + 2 * (i % half), R))

    own_rows = pl.ds(pl.multiple_of(me * PIECE, PIECE), PIECE)
    qp_all[0, own_rows, :] = qp_own[0]

    gk = gk_ref[...].astype(jnp.float32)
    pooled = jnp.concatenate([kpool[0], kpool[1], kpool[2]], axis=1)
    key_gate = fdot(pooled, gk, ((1,), (0,)))
    row16 = lax.broadcasted_iota(jnp.int32, (PIECE, 1), 0)
    qg = jnp.zeros((PIECE, D), jnp.float32)
    for h in range(H):
        t = fdot(qp_own[0], gq_ref[h].astype(jnp.float32), ((1,), (0,)))
        qg = jnp.where(row16 // nb == h, t, qg)
    logits = fdot(qg, key_gate, ((1,), (1,)))

    width = peak.shape[1]
    maps = jnp.full((PIECE, width), NEG, jnp.float32)
    for h in range(H):
        pk = peak[h]
        top = jnp.max(pk, axis=0, keepdims=True)
        total = jnp.sum(bsum[h] * jnp.exp(pk - top), axis=0, keepdims=True)
        chance = (pk - (top + jnp.log(total))).T
        for j in range(nb):
            best = jnp.max(chance[j * BLK:(j + 1) * BLK], axis=0, keepdims=True)
            maps = jnp.where(row16 == h * nb + j, best, maps)
    allowed = maps > 0.1 * NEG
    block_map = jnp.where(allowed, jnp.exp(maps), 0.0)
    for h in range(H):
        for j in range(nb):
            bm_ref[h, j:j + 1, :] = block_map[h * nb + j:h * nb + j + 1, :TB]
    used = row16 < H * nb
    gate_exp = jnp.where(allowed, jnp.exp(logits), 0.0)
    gate_sum = jnp.where(used, jnp.sum(gate_exp, axis=1, keepdims=True), 1.0)
    map_sum = jnp.where(used, jnp.sum(block_map, axis=1, keepdims=True), 1.0)
    diff = gate_exp / gate_sum - block_map / map_sum
    for w in range(width // LANES):
        diff_own[w] = diff[:, w * LANES:(w + 1) * LANES]

    @pl.loop(1, n)
    def _(p):
        small(1, diff_own, diff_all, p).start()

    diff_all[:, own_rows, :] = diff_own[...]

    small_wait(0, qp_all)
    qgs = []
    qps = []
    for h in range(H):
        qp = jnp.concatenate(
            [qp_all[0, pl.ds(h * nb + j, n, stride=PIECE), :] for j in range(nb)], axis=0
        )
        qps.append(qp)
        qgs.append(fdot(qp, gq_ref[h].astype(jnp.float32), ((1,), (0,))))

    small_wait(1, diff_all)
    key_back = jnp.zeros((width, D), jnp.float32)
    for h in range(H):
        parts = []
        for j in range(nb):
            at = pl.ds(h * nb + j, n, stride=PIECE)
            parts.append(jnp.concatenate(
                [diff_all[w, at, :] for w in range(width // LANES)], axis=1
            ))
        diff = jnp.concatenate(parts, axis=0)
        back = fdot(diff, key_gate, ((1,), (0,)))
        dq_ref[h] = fdot(qps[h], back, ((0,), (0,)))
        key_back = key_back + fdot(diff, qgs[h], ((0,), (0,)))
    dk_ref[...] = fdot(pooled, key_back, ((0,), (0,)))

    small_sent(0, qp_all)
    small_sent(1, diff_all)
    for d in range(1, C):
        copy1(d).wait_send()

        @pl.loop(0, half)
        def _(e):
            copy3(d, e).wait_send()

            @pl.when(e > 0)
            def _():
                copy2(d, e).wait_send()


def shards(R, C, queries, keys, doc_ids, gate_query, gate_key):
    H, rows, D = queries.shape
    n = R * C
    nb = rows // BLK
    TB = doc_ids.shape[0]
    width = -(-TB // LANES) * LANES
    half = R // 2
    vm = pl.BlockSpec(memory_space=pltpu.VMEM)
    sm = pl.BlockSpec(memory_space=pltpu.SMEM)
    dma = pltpu.SemaphoreType.DMA
    return pl.pallas_call(
        functools.partial(kernel, R, C),
        out_shape=(
            jax.ShapeDtypeStruct((H, nb, TB), jnp.float32),
            jax.ShapeDtypeStruct((H, D, gate_query.shape[2]), jnp.float32),
            jax.ShapeDtypeStruct(gate_key.shape, jnp.float32),
        ),
        in_specs=[vm, vm, sm, vm, vm],
        out_specs=(vm, vm, vm),
        scratch_shapes=[
            pltpu.VMEM((C * keys.shape[0], D), jnp.bfloat16),
            pltpu.VMEM((D, H * rows), jnp.bfloat16),
            pltpu.VMEM((H, width, rows), jnp.float32),
            pltpu.VMEM((H, width, rows), jnp.float32),
            pltpu.VMEM((3, width, D), jnp.float32),
            pltpu.VMEM((1, PIECE, D), jnp.float32),
            pltpu.VMEM((width // LANES, PIECE, LANES), jnp.float32),
            pltpu.VMEM((1, n * PIECE, D), jnp.float32),
            pltpu.VMEM((width // LANES, n * PIECE, LANES), jnp.float32),
            dma((C,)), dma((C * half,)), dma((C * half,)), dma((n,)),
            dma((2,)), dma((2,)),
        ],
        compiler_params=pltpu.CompilerParams(
            collective_id=0, has_side_effects=True, vmem_limit_bytes=60 * 1024 * 1024
        ),
    )(queries, keys, doc_ids, gate_query, gate_key)


def solution(mesh):
    R, C = mesh.shape["row"], mesh.shape["ctx"]
    in_specs = (P(None, ("row", "ctx"), None), P("ctx", None), P(), P(), P())
    out_specs = (P(None, ("row", "ctx"), None), P(), P())
    return jax.shard_map(
        functools.partial(shards, R, C), mesh=mesh, in_specs=in_specs, out_specs=out_specs,
        check_vma=False,
    )
```

time: 222 us -> 37.8 us (0.17)
  waiting for transfers between devices: 168 us -> 0 us
  Pallas kernels: 0 us -> 33.2 us
  between operations: 15.5 us -> 0.65 us
  loops' own time: 11 us -> 0 us
  other arithmetic: 10.7 us -> 0 us
  local copies, waits for them, and re-layouts: 13.4 us -> 3.71 us
  matrix products: 4.21 us -> 0 us
    psum x1 -> x0, waiting for transfers between devices: 141 us -> none  [shards(): grad_query, grad_key = lax.psum((query_term, key_term), ('row', 'ctx'))]
    pallas_call x0 -> x1, Pallas kernels: none -> 33.2 us  [shards(): pl.pallas_call(functools.partial(kernel, R, C), out_shape=(jax.ShapeDtype...]
    all_gather x1 -> x0, waiting for transfers between devices: 26.4 us -> none  [key_pass(): key_piece = lax.all_gather(key_shard, 'ctx', axis=0, tiled=True)]
    another operation x9 -> x0, loops' own time: 11 us -> none  [the longest x1 10.8 us: key_pass(): lax.fori_loop(0, piece_rows // sub_rows, advance, initial)]
    reduce_max x19 -> x0, other arithmetic: 8.5 us -> none  [the longest x16 7.65 us: pool_keys(): jnp.max(grouped, axis=1)]
    dynamic_slice x9 -> x0, local copies, waits for them, and re-layouts: 4.77 us -> none  [the longest x8 4.69 us: advance(): lax.dynamic_index_in_dim(doc_ids, (key_start + sub_rows - 1) // block_len...]
    dot_general x8 -> x0, matrix products: 4.21 us -> none  [the longest x1 1.43 us: gate_gradients(): jnp.einsum('hbd,hbe->hde', query_pool, query_back, precision=lax.Precisio...]
    gather x2 -> x0, local copies, waits for them, and re-layouts: 2.59 us -> none  [the longest x1 1.29 us: block_docs(): return jnp.repeat(jnp.take(doc_ids, block_starts), block_len)]
  transfers between devices with their start and end apart: 2 -> 0, of which waited for: 2 -> 0; matrix products, arithmetic and copies ran while one was open for 2% -> 0% of each run, Pallas kernels for 0% -> 0%
where the time goes in v1:
time: 37.8 us; the launch traced here: 37.6 us
  Pallas kernels  33.2 us (88%)
  local copies, waits for them, and re-layouts  3.71 us (10%)
  between operations  0.65 us (2%)
    pallas_call x1, Pallas kernels, shards(): pl.pallas_call(functools.partial(kernel, R, C), out_shape=(jax.ShapeDtype...  33.2 us
    unnamed x7, local copies, waits for them, and re-layouts  3.71 us

profile of v1, /device:TPU:0, one launch (start us, length us, event | category | flops | bytes accessed | tf_op | source)
XLA Modules:
  0.0 37.6 jit_solution(3988471897702545355)
XLA Ops:
  0.6 33.2 %shard_map.76 = (f32[5,2,64]{2,1,0:T(2,128)}, f32[5,128,128]{2,1,0:T(8,128)}, f32[384,128]{1,0:T(8,128)}) custom-call(bf16[5,128,128]{2,1,0:T(8,128)(2,1)} %q_ref.1, bf16[1024,128]{1,0:T(8,128)(2,1)} %k_ref.1, s32[64]{0:T(128)} %doc_ref.1, bf16[5,128,128]{2,1,0:T(8,128)(2,1)} %gq_ref.1, bf16[384,128]{1,0:T(8,128)(2,1)} %gk_ref.1), custom_call_target="tpu_custom_call" | custom-call | tf_op jit(solution)/shard_map/pallas_call | solution.py:300
  33.8 0.0 copy-start.1
  33.9 0.7 %copy-done.1 = f32[5,2,64]{2,1,0:T(2,128)S(1)} copy-done((f32[5,2,64]{2,1,0:T(2,128)S(1)}, f32[5,2,64]{2,1,0:T(2,128)}, u32[]{:S(2)}) %copy-start.1) | copy-done | bytes 2584
  34.5 0.6 %copy.11 = f32[5,2,64]{2,1,0:T(2,128)} copy(f32[5,2,64]{2,1,0:T(2,128)S(1)} %copy-done.1) | data formatting | bytes 5120
  35.1 0.0 copy-start
  35.1 1.8 %copy.12 = f32[5,128,128]{2,1,0:T(8,128)} copy(f32[5,128,128]{2,1,0:T(8,128)} %get-tuple-element.7) | data formatting | bytes 655360
  36.9 0.0 copy-done
  36.9 0.7 %copy.13 = f32[384,128]{1,0:T(8,128)} copy(f32[384,128]{1,0:T(8,128)S(1)} %copy-done) | data formatting | bytes 393216
Async XLA Ops:
  33.8 0.7 %copy-start.1 = (f32[5,2,64]{2,1,0:T(2,128)S(1)}, f32[5,2,64]{2,1,0:T(2,128)}, u32[]{:S(2)}) copy-start(f32[5,2,64]{2,1,0:T(2,128)} %get-tuple-element.6) | copy-start | bytes 7684
  35.1 1.8 %copy-start = (f32[384,128]{1,0:T(8,128)S(1)}, f32[384,128]{1,0:T(8,128)}, u32[]{:S(2)}) copy-start(f32[384,128]{1,0:T(8,128)} %get-tuple-element.8) | copy-start | bytes 589828

commit v2 on v1

v2 whole, which is shorter than its diff:
```python
import functools
import math

import jax
import jax.numpy as jnp
from jax import lax
from jax.experimental import pallas as pl
from jax.experimental.pallas import tpu as pltpu
from jax.sharding import PartitionSpec as P

BLK = 64
NEG = -1e30
PIECE = 16
MESH = pl.DeviceIdType.MESH
HI = lax.Precision.HIGHEST


def fdot(a, b, dims):
    return lax.dot_general(a, b, (dims, ((), ())), precision=HI, preferred_element_type=jnp.float32)


def kernel(
    R, C, q_ref, k_ref, doc_ref, gq_ref, gk_ref,
    bm_ref, dq_ref, dk_ref,
    kbuf, q_t, peak, bsum, pieces, diff_own, diff_all,
    s1, s2, s3, rsem, ps1, ps2, ps3, pctx, prow, small_send, small_recv,
):
    H, rows, D = q_ref.shape
    shard = k_ref.shape[0]
    nb = rows // BLK
    n = R * C
    TB = n * nb
    r = lax.axis_index("row")
    c = lax.axis_index("ctx")
    me = r * C + c
    half = R // 2
    scale = 1.0 / math.sqrt(D)
    used = H * nb

    def ctx_peer(d):
        return lax.rem(c + d, C)

    def row_peer(d):
        return lax.rem(r + 2 * d, R)

    partner = r + 1 - 2 * lax.rem(r, 2)

    def other_row(e):
        return lax.rem(partner + 2 * e, R)

    def needs(rr, cc):
        return cc * R < (rr // 2 + 1) * 2 * C

    barrier = pltpu.get_barrier_semaphore()
    for d in range(1, C):
        pl.semaphore_signal(barrier, inc=1, device_id=(r, ctx_peer(d)), device_id_type=MESH)
    for d in range(1, half):
        pl.semaphore_signal(barrier, inc=1, device_id=(row_peer(d), c), device_id_type=MESH)
    pl.semaphore_signal(barrier, inc=1, device_id=(partner, c), device_id_type=MESH)

    def slot(cc, rr):
        return pl.ds(pl.multiple_of(cc * shard + rr * rows, rows), rows)

    def part(rr):
        return pl.ds(pl.multiple_of(rr * PIECE, PIECE), PIECE)

    for h in range(H):
        qf = q_ref[h].astype(jnp.float32)
        q_t[:, h * rows:(h + 1) * rows] = qf.T.astype(jnp.bfloat16)
        for j in range(nb):
            pieces[c, pl.ds(r * PIECE + h * nb + j, 1), :] = jnp.mean(
                qf[j * BLK:(j + 1) * BLK], axis=0, keepdims=True
            )
    wide = k_ref[pl.ds(pl.multiple_of(r * rows, rows), rows), :].astype(jnp.float32)
    for j in range(nb):
        t = wide[j * BLK:(j + 1) * BLK]
        for i, pool in enumerate((jnp.max, jnp.min, jnp.mean)):
            pieces[c, pl.ds(r * PIECE + used + i * nb + j, 1), :] = pool(
                t, axis=0, keepdims=True
            )
    peak[...] = jnp.full_like(peak, NEG)
    bsum[...] = jnp.zeros_like(bsum)

    pl.semaphore_wait(barrier, C - 1 + half)

    def copy1(d):
        return pltpu.make_async_remote_copy(
            src_ref=k_ref.at[pl.ds(pl.multiple_of(r * rows, rows), rows)],
            dst_ref=kbuf.at[slot(c, r)],
            send_sem=s1.at[d], recv_sem=rsem.at[c * R + r],
            device_id=(r, ctx_peer(d)), device_id_type=MESH,
        )

    def copy2(d, e):
        cc = ctx_peer(d)
        return pltpu.make_async_remote_copy(
            src_ref=kbuf.at[slot(cc, r)], dst_ref=kbuf.at[slot(cc, r)],
            send_sem=s2.at[d * half + e], recv_sem=rsem.at[cc * R + r],
            device_id=(row_peer(e), c), device_id_type=MESH,
        )

    def copy3(d, e):
        cc, rr = ctx_peer(d), row_peer(e)
        return pltpu.make_async_remote_copy(
            src_ref=kbuf.at[slot(cc, rr)], dst_ref=kbuf.at[slot(cc, rr)],
            send_sem=s3.at[d * half + e], recv_sem=rsem.at[cc * R + rr],
            device_id=(partner, c), device_id_type=MESH,
        )

    def arrived(cc, rr):
        pltpu.make_async_copy(
            kbuf.at[slot(cc, rr)], kbuf.at[slot(cc, rr)], rsem.at[cc * R + rr]
        ).wait()

    def piece1(d):
        return pltpu.make_async_remote_copy(
            src_ref=pieces.at[c, part(r)], dst_ref=pieces.at[c, part(r)],
            send_sem=ps1.at[d], recv_sem=pctx.at[c],
            device_id=(r, ctx_peer(d)), device_id_type=MESH,
        )

    def piece2(e):
        return pltpu.make_async_remote_copy(
            src_ref=pieces.at[:, part(r)], dst_ref=pieces.at[:, part(r)],
            send_sem=ps2.at[e], recv_sem=prow.at[r],
            device_id=(row_peer(e), c), device_id_type=MESH,
        )

    def piece3(e):
        rr = row_peer(e)
        return pltpu.make_async_remote_copy(
            src_ref=pieces.at[:, part(rr)], dst_ref=pieces.at[:, part(rr)],
            send_sem=ps3.at[e], recv_sem=prow.at[rr],
            device_id=(partner, c), device_id_type=MESH,
        )

    def row_arrived(rr):
        pltpu.make_async_copy(
            pieces.at[:, part(rr)], pieces.at[:, part(rr)], prow.at[rr]
        ).wait()

    for d in range(1, C):
        copy1(d).start()
    for d in range(1, C):
        piece1(d).start()

    a0 = me * nb
    lane = lax.broadcasted_iota(jnp.int32, (1, rows), 1)
    qdoc = jnp.zeros((1, rows), jnp.int32)
    for j in range(nb):
        qdoc = jnp.where(lane // BLK == j, doc_ref[a0 + j], qdoc)

    def score(num, keys, diagonal):
        for h in range(H):
            s = jnp.dot(
                keys, q_t[:, h * rows:(h + 1) * rows], preferred_element_type=jnp.float32
            ) * scale
            if diagonal:
                ki = lax.broadcasted_iota(jnp.int32, (rows, rows), 0)
                qi = lax.broadcasted_iota(jnp.int32, (rows, rows), 1)
                s = jnp.where(ki <= qi, s, NEG)
            for j in range(nb):
                b = num * nb + j
                t = s[j * BLK:(j + 1) * BLK]
                top = jnp.max(t, axis=0, keepdims=True)
                total = jnp.sum(jnp.exp(t - top), axis=0, keepdims=True)
                peak[h, pl.ds(b, 1), :] = jnp.where(qdoc == doc_ref[b], top, NEG)
                bsum[h, pl.ds(b, 1), :] = total

    def process(ref, at, num):
        @pl.when(num < me)
        def _():
            score(num, ref[at, :], False)

        @pl.when(num == me)
        def _():
            score(num, ref[at, :], True)

    @pl.loop(0, R)
    def _(i):
        process(k_ref, pl.ds(pl.multiple_of(i * rows, rows), rows), c * R + i)

    for d in range(1, C):
        cc = ctx_peer(d)
        arrived(cc, r)
        for e in range(1, half):
            @pl.when(needs(row_peer(e), cc))
            def _():
                copy2(d, e).start()

        @pl.when(needs(r, cc))
        def _():
            copy3(d, 0).start()

    for d in range(1, C):
        cc = ctx_peer(d)
        pltpu.make_async_copy(pieces.at[cc, part(r)], pieces.at[cc, part(r)], pctx.at[cc]).wait()
    for e in range(1, half):
        piece2(e).start()
    piece3(0).start()

    @pl.loop(1, C)
    def _(d):
        process(kbuf, slot(ctx_peer(d), r), ctx_peer(d) * R + r)

    @pl.loop(1, C)
    def _(d):
        @pl.when(needs(r, ctx_peer(d)))
        def _():
            @pl.loop(1, half)
            def _(e):
                arrived(ctx_peer(d), row_peer(e))
                copy3(d, e).start()

    for e in range(1, half):
        row_arrived(row_peer(e))
        piece3(e).start()

    @pl.loop(0, (C - 1) * (half - 1))
    def _(i):
        cc, rr = ctx_peer(i // (half - 1) + 1), row_peer(i % (half - 1) + 1)
        process(kbuf, slot(cc, rr), cc * R + rr)

    @pl.loop(0, (C - 1) * half)
    def _(i):
        cc, rr = ctx_peer(i // half + 1), other_row(i % half)

        @pl.when(needs(r, cc))
        def _():
            arrived(cc, rr)

        process(kbuf, slot(cc, rr), cc * R + rr)

    for e in range(half):
        row_arrived(other_row(e))

    def gathered(j):
        return jnp.concatenate(
            [pieces[i, pl.ds(j, R, stride=PIECE), :] for i in range(C)], axis=0
        )

    lanes_k = []
    for i in range(3):
        halves = [gathered(used + i * nb + j) for j in range(nb)]
        lanes_k.append(jnp.stack(halves, axis=1).reshape(TB, D))
    pooled = jnp.concatenate(lanes_k, axis=1)
    key_gate = fdot(pooled, gk_ref[...].astype(jnp.float32), ((1,), (0,)))
    row16 = lax.broadcasted_iota(jnp.int32, (PIECE, 1), 0)
    own = pieces[c, part(r), :]
    qg = jnp.zeros((PIECE, D), jnp.float32)
    qps, qgs = [], []
    for h in range(H):
        gate = gq_ref[h].astype(jnp.float32)
        qg = jnp.where(row16 // nb == h, fdot(own, gate, ((1,), (0,))), qg)
    logits = fdot(qg, key_gate, ((1,), (1,)))

    maps = jnp.full((PIECE, TB), NEG, jnp.float32)
    for h in range(H):
        pk = peak[h]
        top = jnp.max(pk, axis=0, keepdims=True)
        total = jnp.sum(bsum[h] * jnp.exp(pk - top), axis=0, keepdims=True)
        chance = (pk - (top + jnp.log(total))).T
        for j in range(nb):
            best = jnp.max(chance[j * BLK:(j + 1) * BLK], axis=0, keepdims=True)
            maps = jnp.where(row16 == h * nb + j, best, maps)
    allowed = maps > 0.1 * NEG
    block_map = jnp.where(allowed, jnp.exp(maps), 0.0)
    live = row16 < used
    gate_exp = jnp.where(allowed, jnp.exp(logits), 0.0)
    gate_sum = jnp.where(live, jnp.sum(gate_exp, axis=1, keepdims=True), 1.0)
    map_sum = jnp.where(live, jnp.sum(block_map, axis=1, keepdims=True), 1.0)
    diff = gate_exp / gate_sum - block_map / map_sum
    for h in range(H):
        for j in range(nb):
            diff_own[h:h + 1, j * TB:(j + 1) * TB] = diff[h * nb + j:h * nb + j + 1, :]

    place = c * R + r

    def send(p):
        to = lax.rem(place + p, n)
        return pltpu.make_async_remote_copy(
            src_ref=diff_own, dst_ref=diff_all.at[place],
            send_sem=small_send.at[0], recv_sem=small_recv.at[0],
            device_id=(to % R, to // R), device_id_type=MESH,
        )

    @pl.loop(1, n)
    def _(p):
        send(p).start()

    diff_all[place] = diff_own[...]
    for h in range(H):
        for j in range(nb):
            bm_ref[h, j:j + 1, :] = block_map[h * nb + j:h * nb + j + 1, :]

    for h in range(H):
        qp = jnp.concatenate([gathered(h * nb + j) for j in range(nb)], axis=0)
        qps.append(qp)
        qgs.append(fdot(qp, gq_ref[h].astype(jnp.float32), ((1,), (0,))))

    both = jnp.concatenate([key_gate] * nb, axis=0)
    wide_lane = lax.broadcasted_iota(jnp.int32, (1, nb * TB), 1)
    rest = diff_all.at[pl.ds(0, n - 1)]
    pltpu.make_async_copy(rest, rest, small_recv.at[0]).wait()
    key_back = jnp.zeros((nb * TB, D), jnp.float32)
    for h in range(H):
        mixed = diff_all[:, h, :]
        diff = jnp.concatenate(
            [jnp.where(wide_lane // TB == j, mixed, 0.0) for j in range(nb)], axis=0
        )
        back = fdot(diff, both, ((1,), (0,)))
        dq_ref[h] = fdot(qps[h], back, ((0,), (0,)))
        key_back = key_back + fdot(diff, qgs[h], ((0,), (0,)))
    folded = key_back[:TB]
    for j in range(1, nb):
        folded = folded + key_back[j * TB:(j + 1) * TB]
    dk_ref[...] = fdot(pooled, folded, ((0,), (0,)))

    pltpu.make_async_copy(rest, rest, small_send.at[0]).wait()
    for d in range(1, C):
        cc = ctx_peer(d)
        copy1(d).wait_send()
        piece1(d).wait_send()
        for e in range(half):
            @pl.when(needs(r, cc))
            def _():
                copy3(d, e).wait_send()

            if e > 0:
                @pl.when(needs(row_peer(e), cc))
                def _():
                    copy2(d, e).wait_send()
    for e in range(half):
        piece3(e).wait_send()
        if e > 0:
            piece2(e).wait_send()


def shards(R, C, queries, keys, doc_ids, gate_query, gate_key):
    H, rows, D = queries.shape
    n = R * C
    nb = rows // BLK
    TB = doc_ids.shape[0]
    half = R // 2
    vm = pl.BlockSpec(memory_space=pltpu.VMEM)
    sm = pl.BlockSpec(memory_space=pltpu.SMEM)
    dma = pltpu.SemaphoreType.DMA
    return pl.pallas_call(
        functools.partial(kernel, R, C),
        out_shape=(
            jax.ShapeDtypeStruct((H, nb, TB), jnp.float32),
            jax.ShapeDtypeStruct((H, D, gate_query.shape[2]), jnp.float32),
            jax.ShapeDtypeStruct(gate_key.shape, jnp.float32),
        ),
        in_specs=[vm, vm, sm, vm, vm],
        out_specs=(vm, vm, vm),
        scratch_shapes=[
            pltpu.VMEM((C * keys.shape[0], D), jnp.bfloat16),
            pltpu.VMEM((D, H * rows), jnp.bfloat16),
            pltpu.VMEM((H, TB, rows), jnp.float32),
            pltpu.VMEM((H, TB, rows), jnp.float32),
            pltpu.VMEM((C, R * PIECE, D), jnp.float32),
            pltpu.VMEM((H, nb * TB), jnp.float32),
            pltpu.VMEM((n, H, nb * TB), jnp.float32),
            dma((C,)), dma((C * half,)), dma((C * half,)), dma((n,)),
            dma((C,)), dma((half,)), dma((half,)), dma((C,)), dma((R,)),
            dma((1,)), dma((1,)),
        ],
        compiler_params=pltpu.CompilerParams(
            collective_id=0, has_side_effects=True, vmem_limit_bytes=60 * 1024 * 1024
        ),
    )(queries, keys, doc_ids, gate_query, gate_key)


def solution(mesh):
    R, C = mesh.shape["row"], mesh.shape["ctx"]
    in_specs = (P(None, ("row", "ctx"), None), P("ctx", None), P(), P(), P())
    out_specs = (P(None, ("row", "ctx"), None), P(), P())
    return jax.shard_map(
        functools.partial(shards, R, C), mesh=mesh, in_specs=in_specs, out_specs=out_specs,
        check_vma=False,
    )
```

time: 37.8 us -> 37.1 us (0.981)
  Pallas kernels: 33.2 us -> 32.6 us
    pallas_call x1, Pallas kernels: 33.2 us -> 32.6 us  [shards(): pl.pallas_call(functools.partial(kernel, R, C), out_shape=(jax.ShapeDtype...]
where the time goes in v2:
time: 37.1 us; the launch traced here: 37 us
  Pallas kernels  32.6 us (88%)
  local copies, waits for them, and re-layouts  3.71 us (10%)
  between operations  0.65 us (2%)
    pallas_call x1, Pallas kernels, shards(): pl.pallas_call(functools.partial(kernel, R, C), out_shape=(jax.ShapeDtype...  32.6 us
    unnamed x7, local copies, waits for them, and re-layouts  3.71 us

profile of v2, /device:TPU:0, one launch (start us, length us, event | category | flops | bytes accessed | tf_op | source)
XLA Modules:
  0.0 37.0 jit_solution(10972017019373737487)
XLA Ops:
  0.6 32.6 %shard_map.76 = (f32[5,2,64]{2,1,0:T(2,128)}, f32[5,128,128]{2,1,0:T(8,128)}, f32[384,128]{1,0:T(8,128)}) custom-call(bf16[5,128,128]{2,1,0:T(8,128)(2,1)} %q_ref.1, bf16[1024,128]{1,0:T(8,128)(2,1)} %k_ref.1, s32[64]{0:T(128)} %doc_ref.1, bf16[5,128,128]{2,1,0:T(8,128)(2,1)} %gq_ref.1, bf16[384,128]{1,0:T(8,128)(2,1)} %gk_ref.1), custom_call_target="tpu_custom_call" | custom-call | tf_op jit(solution)/shard_map/pallas_call | solution.py:348
  33.2 0.0 copy-start.1
  33.2 0.7 %copy-done.1 = f32[5,2,64]{2,1,0:T(2,128)S(1)} copy-done((f32[5,2,64]{2,1,0:T(2,128)S(1)}, f32[5,2,64]{2,1,0:T(2,128)}, u32[]{:S(2)}) %copy-start.1) | copy-done | bytes 2584
  33.9 0.6 %copy.11 = f32[5,2,64]{2,1,0:T(2,128)} copy(f32[5,2,64]{2,1,0:T(2,128)S(1)} %copy-done.1) | data formatting | bytes 5120
  34.5 0.0 copy-start
  34.5 1.8 %copy.12 = f32[5,128,128]{2,1,0:T(8,128)} copy(f32[5,128,128]{2,1,0:T(8,128)} %get-tuple-element.7) | data formatting | bytes 655360
  36.3 0.0 copy-done
  36.3 0.7 %copy.13 = f32[384,128]{1,0:T(8,128)} copy(f32[384,128]{1,0:T(8,128)S(1)} %copy-done) | data formatting | bytes 393216
Async XLA Ops:
  33.2 0.7 %copy-start.1 = (f32[5,2,64]{2,1,0:T(2,128)S(1)}, f32[5,2,64]{2,1,0:T(2,128)}, u32[]{:S(2)}) copy-start(f32[5,2,64]{2,1,0:T(2,128)} %get-tuple-element.6) | copy-start | bytes 7684
  34.5 1.8 %copy-start = (f32[384,128]{1,0:T(8,128)S(1)}, f32[384,128]{1,0:T(8,128)}, u32[]{:S(2)}) copy-start(f32[384,128]{1,0:T(8,128)} %get-tuple-element.8) | copy-start | bytes 589828

commit v3 on v2

--- a/solution.py
+++ b/solution.py
@@ -11,6 +11,7 @@
 BLK = 64
 NEG = -1e30
 PIECE = 16
+GROUP = 4
 MESH = pl.DeviceIdType.MESH
 HI = lax.Precision.HIGHEST
 
@@ -23,7 +24,7 @@
     R, C, q_ref, k_ref, doc_ref, gq_ref, gk_ref,
     bm_ref, dq_ref, dk_ref,
     kbuf, q_t, peak, bsum, pieces, diff_own, diff_all,
-    s1, s2, s3, rsem, ps1, ps2, ps3, pctx, prow, small_send, small_recv,
+    s1, s2, s3, rsem, ps1, ps2, ps3, pctx, prow, ds1, ds2, dctx, drow,
 ):
     H, rows, D = q_ref.shape
     shard = k_ref.shape[0]
@@ -81,69 +82,6 @@
     peak[...] = jnp.full_like(peak, NEG)
     bsum[...] = jnp.zeros_like(bsum)
 
-    pl.semaphore_wait(barrier, C - 1 + half)
-
-    def copy1(d):
-        return pltpu.make_async_remote_copy(
-            src_ref=k_ref.at[pl.ds(pl.multiple_of(r * rows, rows), rows)],
-            dst_ref=kbuf.at[slot(c, r)],
-            send_sem=s1.at[d], recv_sem=rsem.at[c * R + r],
-            device_id=(r, ctx_peer(d)), device_id_type=MESH,
-        )
-
-    def copy2(d, e):
-        cc = ctx_peer(d)
-        return pltpu.make_async_remote_copy(
-            src_ref=kbuf.at[slot(cc, r)], dst_ref=kbuf.at[slot(cc, r)],
-            send_sem=s2.at[d * half + e], recv_sem=rsem.at[cc * R + r],
-            device_id=(row_peer(e), c), device_id_type=MESH,
-        )
-
-    def copy3(d, e):
-        cc, rr = ctx_peer(d), row_peer(e)
-        return pltpu.make_async_remote_copy(
-            src_ref=kbuf.at[slot(cc, rr)], dst_ref=kbuf.at[slot(cc, rr)],
-            send_sem=s3.at[d * half + e], recv_sem=rsem.at[cc * R + rr],
-            device_id=(partner, c), device_id_type=MESH,
-        )
-
-    def arrived(cc, rr):
-        pltpu.make_async_copy(
-            kbuf.at[slot(cc, rr)], kbuf.at[slot(cc, rr)], rsem.at[cc * R + rr]
-        ).wait()
-
-    def piece1(d):
-        return pltpu.make_async_remote_copy(
-            src_ref=pieces.at[c, part(r)], dst_ref=pieces.at[c, part(r)],
-            send_sem=ps1.at[d], recv_sem=pctx.at[c],
-            device_id=(r, ctx_peer(d)), device_id_type=MESH,
-        )
-
-    def piece2(e):
-        return pltpu.make_async_remote_copy(
-            src_ref=pieces.at[:, part(r)], dst_ref=pieces.at[:, part(r)],
-            send_sem=ps2.at[e], recv_sem=prow.at[r],
-            device_id=(row_peer(e), c), device_id_type=MESH,
-        )
-
-    def piece3(e):
-        rr = row_peer(e)
-        return pltpu.make_async_remote_copy(
-            src_ref=pieces.at[:, part(rr)], dst_ref=pieces.at[:, part(rr)],
-            send_sem=ps3.at[e], recv_sem=prow.at[rr],
-            device_id=(partner, c), device_id_type=MESH,
-        )
-
-    def row_arrived(rr):
-        pltpu.make_async_copy(
-            pieces.at[:, part(rr)], pieces.at[:, part(rr)], prow.at[rr]
-        ).wait()
-
-    for d in range(1, C):
-        copy1(d).start()
-    for d in range(1, C):
-        piece1(d).start()
-
     a0 = me * nb
     lane = lax.broadcasted_iota(jnp.int32, (1, rows), 1)
     qdoc = jnp.zeros((1, rows), jnp.int32)
@@ -154,31 +92,110 @@
         for h in range(H):
             s = jnp.dot(
                 keys, q_t[:, h * rows:(h + 1) * rows], preferred_element_type=jnp.float32
-            ) * scale
+            )
             if diagonal:
                 ki = lax.broadcasted_iota(jnp.int32, (rows, rows), 0)
                 qi = lax.broadcasted_iota(jnp.int32, (rows, rows), 1)
                 s = jnp.where(ki <= qi, s, NEG)
-            for j in range(nb):
+            for j in range(keys.shape[0] // BLK):
                 b = num * nb + j
                 t = s[j * BLK:(j + 1) * BLK]
                 top = jnp.max(t, axis=0, keepdims=True)
-                total = jnp.sum(jnp.exp(t - top), axis=0, keepdims=True)
-                peak[h, pl.ds(b, 1), :] = jnp.where(qdoc == doc_ref[b], top, NEG)
+                total = jnp.sum(
+                    jnp.exp2((t - top) * (scale * math.log2(math.e))), axis=0, keepdims=True
+                )
+                peak[h, pl.ds(b, 1), :] = jnp.where(qdoc == doc_ref[b], top * scale, NEG)
                 bsum[h, pl.ds(b, 1), :] = total
 
-    def process(ref, at, num):
-        @pl.when(num < me)
-        def _():
-            score(num, ref[at, :], False)
-
-        @pl.when(num == me)
-        def _():
-            score(num, ref[at, :], True)
-
-    @pl.loop(0, R)
-    def _(i):
-        process(k_ref, pl.ds(pl.multiple_of(i * rows, rows), rows), c * R + i)
+    group = math.gcd(R, GROUP)
+
+    def process(ref, base, first):
+        @pl.when(first + group <= me)
+        def _():
+            for i in range(0, group, 2):
+                at = pl.multiple_of(base + i * rows, rows)
+                score(first + i, ref[pl.ds(at, 2 * rows), :], False)
+
+        @pl.when(first + group > me)
+        def _():
+            @pl.loop(0, group)
+            def _(i):
+                at = pl.ds(pl.multiple_of(base + i * rows, rows), rows)
+
+                @pl.when(first + i < me)
+                def _():
+                    score(first + i, ref[at, :], False)
+
+                @pl.when(first + i == me)
+                def _():
+                    score(first + i, ref[at, :], True)
+
+    @pl.loop(0, R // group)
+    def _(g):
+        process(k_ref, g * group * rows, c * R + g * group)
+
+    pl.semaphore_wait(barrier, C - 1 + half)
+
+    def copy1(d):
+        return pltpu.make_async_remote_copy(
+            src_ref=k_ref.at[pl.ds(pl.multiple_of(r * rows, rows), rows)],
+            dst_ref=kbuf.at[slot(c, r)],
+            send_sem=s1.at[d], recv_sem=rsem.at[c * R + r],
+            device_id=(r, ctx_peer(d)), device_id_type=MESH,
+        )
+
+    def copy2(d, e):
+        cc = ctx_peer(d)
+        return pltpu.make_async_remote_copy(
+            src_ref=kbuf.at[slot(cc, r)], dst_ref=kbuf.at[slot(cc, r)],
+            send_sem=s2.at[d * half + e], recv_sem=rsem.at[cc * R + r],
+            device_id=(row_peer(e), c), device_id_type=MESH,
+        )
+
+    def copy3(d, e):
+        cc, rr = ctx_peer(d), row_peer(e)
+        return pltpu.make_async_remote_copy(
+            src_ref=kbuf.at[slot(cc, rr)], dst_ref=kbuf.at[slot(cc, rr)],
+            send_sem=s3.at[d * half + e], recv_sem=rsem.at[cc * R + rr],
+            device_id=(partner, c), device_id_type=MESH,
+        )
+
+    def arrived(cc, rr):
+        pltpu.make_async_copy(
+            kbuf.at[slot(cc, rr)], kbuf.at[slot(cc, rr)], rsem.at[cc * R + rr]
+        ).wait()
+
+    def piece1(d):
+        return pltpu.make_async_remote_copy(
+            src_ref=pieces.at[c, part(r)], dst_ref=pieces.at[c, part(r)],
+            send_sem=ps1.at[d], recv_sem=pctx.at[c],
+            device_id=(r, ctx_peer(d)), device_id_type=MESH,
+        )
+
+    def piece2(e):
+        return pltpu.make_async_remote_copy(
+            src_ref=pieces.at[:, part(r)], dst_ref=pieces.at[:, part(r)],
+            send_sem=ps2.at[e], recv_sem=prow.at[r],
+            device_id=(row_peer(e), c), device_id_type=MESH,
+        )
+
+    def piece3(e):
+        rr = row_peer(e)
+        return pltpu.make_async_remote_copy(
+            src_ref=pieces.at[:, part(rr)], dst_ref=pieces.at[:, part(rr)],
+            send_sem=ps3.at[e], recv_sem=prow.at[rr],
+            device_id=(partner, c), device_id_type=MESH,
+        )
+
+    def row_arrived(rr):
+        pltpu.make_async_copy(
+            pieces.at[:, part(rr)], pieces.at[:, part(rr)], prow.at[rr]
+        ).wait()
+
+    for d in range(1, C):
+        copy1(d).start()
+    for d in range(1, C):
+        piece1(d).start()
 
     for d in range(1, C):
         cc = ctx_peer(d)
@@ -201,10 +218,6 @@
 
     @pl.loop(1, C)
     def _(d):
-        process(kbuf, slot(ctx_peer(d), r), ctx_peer(d) * R + r)
-
-    @pl.loop(1, C)
-    def _(d):
         @pl.when(needs(r, ctx_peer(d)))
         def _():
             @pl.loop(1, half)
@@ -216,20 +229,19 @@
         row_arrived(row_peer(e))
         piece3(e).start()
 
-    @pl.loop(0, (C - 1) * (half - 1))
-    def _(i):
-        cc, rr = ctx_peer(i // (half - 1) + 1), row_peer(i % (half - 1) + 1)
-        process(kbuf, slot(cc, rr), cc * R + rr)
-
-    @pl.loop(0, (C - 1) * half)
-    def _(i):
-        cc, rr = ctx_peer(i // half + 1), other_row(i % half)
+    @pl.loop(1, C)
+    def _(d):
+        cc = ctx_peer(d)
 
         @pl.when(needs(r, cc))
         def _():
-            arrived(cc, rr)
-
-        process(kbuf, slot(cc, rr), cc * R + rr)
+            @pl.loop(0, half)
+            def _(e):
+                arrived(cc, other_row(e))
+
+            @pl.loop(0, R // group)
+            def _(g):
+                process(kbuf, cc * shard + g * group * rows, cc * R + g * group)
 
     for e in range(half):
         row_arrived(other_row(e))
@@ -263,7 +275,7 @@
         for j in range(nb):
             best = jnp.max(chance[j * BLK:(j + 1) * BLK], axis=0, keepdims=True)
             maps = jnp.where(row16 == h * nb + j, best, maps)
-    allowed = maps > 0.1 * NEG
+    allowed = maps > 0.01 * NEG
     block_map = jnp.where(allowed, jnp.exp(maps), 0.0)
     live = row16 < used
     gate_exp = jnp.where(allowed, jnp.exp(logits), 0.0)
@@ -274,24 +286,25 @@
         for j in range(nb):
             diff_own[h:h + 1, j * TB:(j + 1) * TB] = diff[h * nb + j:h * nb + j + 1, :]
 
-    place = c * R + r
-
-    def send(p):
-        to = lax.rem(place + p, n)
-        return pltpu.make_async_remote_copy(
-            src_ref=diff_own, dst_ref=diff_all.at[place],
-            send_sem=small_send.at[0], recv_sem=small_recv.at[0],
-            device_id=(to % R, to // R), device_id_type=MESH,
-        )
-
-    @pl.loop(1, n)
-    def _(p):
-        send(p).start()
-
-    diff_all[place] = diff_own[...]
+    def send(d, e):
+        to_row, to_ctx = r + e, c + d
+        to_row = jnp.where(to_row >= R, to_row - R, to_row)
+        to_ctx = jnp.where(to_ctx >= C, to_ctx - C, to_ctx)
+        return pltpu.make_async_remote_copy(
+            src_ref=diff_own, dst_ref=diff_all.at[c * R + r],
+            send_sem=ds1.at[0], recv_sem=dctx.at[0],
+            device_id=(to_row, to_ctx), device_id_type=MESH,
+        )
+
+    for e in range(R - 1, -1, -1):
+        for d in range(C - 1, -1, -1):
+            if d or e:
+                send(d, e).start()
+    diff_all[c * R + r] = diff_own[...]
     for h in range(H):
         for j in range(nb):
             bm_ref[h, j:j + 1, :] = block_map[h * nb + j:h * nb + j + 1, :]
+
 
     for h in range(H):
         qp = jnp.concatenate([gathered(h * nb + j) for j in range(nb)], axis=0)
@@ -301,7 +314,7 @@
     both = jnp.concatenate([key_gate] * nb, axis=0)
     wide_lane = lax.broadcasted_iota(jnp.int32, (1, nb * TB), 1)
     rest = diff_all.at[pl.ds(0, n - 1)]
-    pltpu.make_async_copy(rest, rest, small_recv.at[0]).wait()
+    pltpu.make_async_copy(rest, rest, dctx.at[0]).wait()
     key_back = jnp.zeros((nb * TB, D), jnp.float32)
     for h in range(H):
         mixed = diff_all[:, h, :]
@@ -316,7 +329,7 @@
         folded = folded + key_back[j * TB:(j + 1) * TB]
     dk_ref[...] = fdot(pooled, folded, ((0,), (0,)))
 
-    pltpu.make_async_copy(rest, rest, small_send.at[0]).wait()
+    pltpu.make_async_copy(rest, rest, ds1.at[0]).wait()
     for d in range(1, C):
         cc = ctx_peer(d)
         copy1(d).wait_send()
@@ -364,7 +377,7 @@
             pltpu.VMEM((n, H, nb * TB), jnp.float32),
             dma((C,)), dma((C * half,)), dma((C * half,)), dma((n,)),
             dma((C,)), dma((half,)), dma((half,)), dma((C,)), dma((R,)),
-            dma((1,)), dma((1,)),
+            dma((C,)), dma((R,)), dma((C,)), dma((R,)),
         ],
         compiler_params=pltpu.CompilerParams(
             collective_id=0, has_side_effects=True, vmem_limit_bytes=60 * 1024 * 1024

time: 37.1 us -> 34.9 us (0.941)
  Pallas kernels: 32.6 us -> 30.3 us
    pallas_call x1, Pallas kernels: 32.6 us -> 30.3 us  [shards(): pl.pallas_call(functools.partial(kernel, R, C), out_shape=(jax.ShapeDtype...]
where the time goes in v3:
time: 34.9 us; the launch traced here: 34.7 us
  Pallas kernels  30.3 us (87%)
  local copies, waits for them, and re-layouts  3.71 us (11%)
  between operations  0.65 us (2%)
    pallas_call x1, Pallas kernels, shards(): pl.pallas_call(functools.partial(kernel, R, C), out_shape=(jax.ShapeDtype...  30.3 us
    unnamed x7, local copies, waits for them, and re-layouts  3.71 us

profile of v3, /device:TPU:0, one launch (start us, length us, event | category | flops | bytes accessed | tf_op | source)
XLA Modules:
  0.0 34.7 jit_solution(12627591816235034468)
XLA Ops:
  0.6 30.3 %shard_map.76 = (f32[5,2,64]{2,1,0:T(2,128)}, f32[5,128,128]{2,1,0:T(8,128)}, f32[384,128]{1,0:T(8,128)}) custom-call(bf16[5,128,128]{2,1,0:T(8,128)(2,1)} %q_ref.1, bf16[1024,128]{1,0:T(8,128)(2,1)} %k_ref.1, s32[64]{0:T(128)} %doc_ref.1, bf16[5,128,128]{2,1,0:T(8,128)(2,1)} %gq_ref.1, bf16[384,128]{1,0:T(8,128)(2,1)} %gk_ref.1), custom_call_target="tpu_custom_call" | custom-call | tf_op jit(solution)/shard_map/pallas_call | solution.py:361
  31.0 0.0 copy-start.1
  31.0 0.7 %copy-done.1 = f32[5,2,64]{2,1,0:T(2,128)S(1)} copy-done((f32[5,2,64]{2,1,0:T(2,128)S(1)}, f32[5,2,64]{2,1,0:T(2,128)}, u32[]{:S(2)}) %copy-start.1) | copy-done | bytes 2584
  31.7 0.6 %copy.11 = f32[5,2,64]{2,1,0:T(2,128)} copy(f32[5,2,64]{2,1,0:T(2,128)S(1)} %copy-done.1) | data formatting | bytes 5120
  32.2 0.0 copy-start
  32.2 1.8 %copy.12 = f32[5,128,128]{2,1,0:T(8,128)} copy(f32[5,128,128]{2,1,0:T(8,128)} %get-tuple-element.7) | data formatting | bytes 655360
  34.0 0.0 copy-done
  34.0 0.7 %copy.13 = f32[384,128]{1,0:T(8,128)} copy(f32[384,128]{1,0:T(8,128)S(1)} %copy-done) | data formatting | bytes 393216
Async XLA Ops:
  31.0 0.7 %copy-start.1 = (f32[5,2,64]{2,1,0:T(2,128)S(1)}, f32[5,2,64]{2,1,0:T(2,128)}, u32[]{:S(2)}) copy-start(f32[5,2,64]{2,1,0:T(2,128)} %get-tuple-element.6) | copy-start | bytes 7684
  32.2 1.8 %copy-start = (f32[384,128]{1,0:T(8,128)S(1)}, f32[384,128]{1,0:T(8,128)}, u32[]{:S(2)}) copy-start(f32[384,128]{1,0:T(8,128)} %get-tuple-element.8) | copy-start | bytes 589828

commit v4 on v3

--- a/solution.py
+++ b/solution.py
@@ -22,7 +22,7 @@
 
 def kernel(
     R, C, q_ref, k_ref, doc_ref, gq_ref, gk_ref,
-    bm_ref, dq_ref, dk_ref,
+    bm_ref, qp_ref, qg_ref, both_ref, pooled_ref, diff_ref,
     kbuf, q_t, peak, bsum, pieces, diff_own, diff_all,
     s1, s2, s3, rsem, ps1, ps2, ps3, pctx, prow, ds1, ds2, dctx, drow,
 ):
@@ -193,9 +193,16 @@
         ).wait()
 
     for d in range(1, C):
+        piece1(d).start()
+    for d in range(1, C):
         copy1(d).start()
-    for d in range(1, C):
-        piece1(d).start()
+
+    for d in range(1, C):
+        cc = ctx_peer(d)
+        pltpu.make_async_copy(pieces.at[cc, part(r)], pieces.at[cc, part(r)], pctx.at[cc]).wait()
+    for e in range(1, half):
+        piece2(e).start()
+    piece3(0).start()
 
     for d in range(1, C):
         cc = ctx_peer(d)
@@ -209,12 +216,9 @@
         def _():
             copy3(d, 0).start()
 
-    for d in range(1, C):
-        cc = ctx_peer(d)
-        pltpu.make_async_copy(pieces.at[cc, part(r)], pieces.at[cc, part(r)], pctx.at[cc]).wait()
     for e in range(1, half):
-        piece2(e).start()
-    piece3(0).start()
+        row_arrived(row_peer(e))
+        piece3(e).start()
 
     @pl.loop(1, C)
     def _(d):
@@ -224,24 +228,6 @@
             def _(e):
                 arrived(ctx_peer(d), row_peer(e))
                 copy3(d, e).start()
-
-    for e in range(1, half):
-        row_arrived(row_peer(e))
-        piece3(e).start()
-
-    @pl.loop(1, C)
-    def _(d):
-        cc = ctx_peer(d)
-
-        @pl.when(needs(r, cc))
-        def _():
-            @pl.loop(0, half)
-            def _(e):
-                arrived(cc, other_row(e))
-
-            @pl.loop(0, R // group)
-            def _(g):
-                process(kbuf, cc * shard + g * group * rows, cc * R + g * group)
 
     for e in range(half):
         row_arrived(other_row(e))
@@ -260,11 +246,24 @@
     row16 = lax.broadcasted_iota(jnp.int32, (PIECE, 1), 0)
     own = pieces[c, part(r), :]
     qg = jnp.zeros((PIECE, D), jnp.float32)
-    qps, qgs = [], []
     for h in range(H):
         gate = gq_ref[h].astype(jnp.float32)
         qg = jnp.where(row16 // nb == h, fdot(own, gate, ((1,), (0,))), qg)
     logits = fdot(qg, key_gate, ((1,), (1,)))
+
+    @pl.loop(1, C)
+    def _(d):
+        cc = ctx_peer(d)
+
+        @pl.when(needs(r, cc))
+        def _():
+            @pl.loop(0, half)
+            def _(e):
+                arrived(cc, other_row(e))
+
+            @pl.loop(0, R // group)
+            def _(g):
+                process(kbuf, cc * shard + g * group * rows, cc * R + g * group)
 
     maps = jnp.full((PIECE, TB), NEG, jnp.float32)
     for h in range(H):
@@ -308,27 +307,15 @@
 
     for h in range(H):
         qp = jnp.concatenate([gathered(h * nb + j) for j in range(nb)], axis=0)
-        qps.append(qp)
-        qgs.append(fdot(qp, gq_ref[h].astype(jnp.float32), ((1,), (0,))))
-
-    both = jnp.concatenate([key_gate] * nb, axis=0)
-    wide_lane = lax.broadcasted_iota(jnp.int32, (1, nb * TB), 1)
+        qp_ref[h] = qp
+        qg_ref[h] = fdot(qp, gq_ref[h].astype(jnp.float32), ((1,), (0,)))
+
+    for j in range(nb):
+        both_ref[j * TB:(j + 1) * TB] = key_gate
+    pooled_ref[...] = pooled
     rest = diff_all.at[pl.ds(0, n - 1)]
     pltpu.make_async_copy(rest, rest, dctx.at[0]).wait()
-    key_back = jnp.zeros((nb * TB, D), jnp.float32)
-    for h in range(H):
-        mixed = diff_all[:, h, :]
-        diff = jnp.concatenate(
-            [jnp.where(wide_lane // TB == j, mixed, 0.0) for j in range(nb)], axis=0
-        )
-        back = fdot(diff, both, ((1,), (0,)))
-        dq_ref[h] = fdot(qps[h], back, ((0,), (0,)))
-        key_back = key_back + fdot(diff, qgs[h], ((0,), (0,)))
-    folded = key_back[:TB]
-    for j in range(1, nb):
-        folded = folded + key_back[j * TB:(j + 1) * TB]
-    dk_ref[...] = fdot(pooled, folded, ((0,), (0,)))
-
+    diff_ref[...] = diff_all[...]
     pltpu.make_async_copy(rest, rest, ds1.at[0]).wait()
     for d in range(1, C):
         cc = ctx_peer(d)
@@ -347,6 +334,26 @@
         piece3(e).wait_send()
         if e > 0:
             piece2(e).wait_send()
+
+
+def finish(map_ref, qp_ref, qg_ref, both_ref, pooled_ref, diff_ref, bm_ref, dq_ref, dk_ref):
+    H, nb, TB = map_ref.shape
+    bm_ref[...] = map_ref[...]
+    both = both_ref[...]
+    wide_lane = lax.broadcasted_iota(jnp.int32, (1, nb * TB), 1)
+    key_back = jnp.zeros(both.shape, jnp.float32)
+    for h in range(H):
+        mixed = diff_ref[:, h, :]
+        diff = jnp.concatenate(
+            [jnp.where(wide_lane // TB == j, mixed, 0.0) for j in range(nb)], axis=0
+        )
+        back = fdot(diff, both, ((1,), (0,)))
+        dq_ref[h] = fdot(qp_ref[h], back, ((0,), (0,)))
+        key_back = key_back + fdot(diff, qg_ref[h], ((0,), (0,)))
+    folded = key_back[:TB]
+    for j in range(1, nb):
+        folded = folded + key_back[j * TB:(j + 1) * TB]
+    dk_ref[...] = fdot(pooled_ref[...], folded, ((0,), (0,)))
 
 
 def shards(R, C, queries, keys, doc_ids, gate_query, gate_key):
@@ -358,15 +365,18 @@
     vm = pl.BlockSpec(memory_space=pltpu.VMEM)
     sm = pl.BlockSpec(memory_space=pltpu.SMEM)
     dma = pltpu.SemaphoreType.DMA
-    return pl.pallas_call(
+    parts = pl.pallas_call(
         functools.partial(kernel, R, C),
         out_shape=(
             jax.ShapeDtypeStruct((H, nb, TB), jnp.float32),
-            jax.ShapeDtypeStruct((H, D, gate_query.shape[2]), jnp.float32),
-            jax.ShapeDtypeStruct(gate_key.shape, jnp.float32),
+            jax.ShapeDtypeStruct((H, nb * n, D), jnp.float32),
+            jax.ShapeDtypeStruct((H, nb * n, D), jnp.float32),
+            jax.ShapeDtypeStruct((nb * TB, D), jnp.float32),
+            jax.ShapeDtypeStruct((TB, 3 * D), jnp.float32),
+            jax.ShapeDtypeStruct((n, H, nb * TB), jnp.float32),
         ),
         in_specs=[vm, vm, sm, vm, vm],
-        out_specs=(vm, vm, vm),
+        out_specs=(vm,) * 6,
         scratch_shapes=[
             pltpu.VMEM((C * keys.shape[0], D), jnp.bfloat16),
             pltpu.VMEM((D, H * rows), jnp.bfloat16),
@@ -383,6 +393,17 @@
             collective_id=0, has_side_effects=True, vmem_limit_bytes=60 * 1024 * 1024
         ),
     )(queries, keys, doc_ids, gate_query, gate_key)
+    return pl.pallas_call(
+        finish,
+        out_shape=(
+            jax.ShapeDtypeStruct((H, nb, TB), jnp.float32),
+            jax.ShapeDtypeStruct(gate_query.shape, jnp.float32),
+            jax.ShapeDtypeStruct(gate_key.shape, jnp.float32),
+        ),
+        in_specs=[vm] * 6,
+        out_specs=(vm,) * 3,
+        compiler_params=pltpu.CompilerParams(vmem_limit_bytes=60 * 1024 * 1024),
+    )(*parts)
 
 
 def solution(mesh):

time: 34.9 us -> 33.2 us (0.951)
  local copies, waits for them, and re-layouts: 3.71 us -> 0 us
  Pallas kernels: 30.3 us -> 32.4 us
    pallas_call x0 -> x1, Pallas kernels: none -> 3.99 us  [shards(): pl.pallas_call(finish, out_shape=(jax.ShapeDtypeStruct((H, nb, TB), jnp.f...]
    unnamed x7 -> x0, local copies, waits for them, and re-layouts: 3.71 us -> none
    pallas_call x1, Pallas kernels: 30.3 us -> 28.4 us  [shards(): pl.pallas_call(functools.partial(kernel, R, C), out_shape=(jax.ShapeDtype...]
where the time goes in v4:
time: 33.2 us; the launch traced here: 33.1 us
  Pallas kernels  32.4 us (98%)
  between operations  0.64 us (2%)
    pallas_call x1, Pallas kernels, shards(): pl.pallas_call(functools.partial(kernel, R, C), out_shape=(jax.ShapeDtype...  28.4 us
    pallas_call x1, Pallas kernels, shards(): pl.pallas_call(finish, out_shape=(jax.ShapeDtypeStruct((H, nb, TB), jnp.f...  3.99 us

profile of v4, /device:TPU:0, one launch (start us, length us, event | category | flops | bytes accessed | tf_op | source)
XLA Modules:
  0.0 33.1 jit_solution(11479078225816048906)
XLA Ops:
  0.6 28.4 %shard_map.76 = (f32[5,2,64]{2,1,0:T(2,128)}, f32[5,64,128]{2,1,0:T(8,128)}, f32[5,64,128]{2,1,0:T(8,128)}, f32[128,128]{1,0:T(8,128)}, f32[64,384]{1,0:T(8,128)}, /*index=5*/f32[32,5,128]{2,1,0:T(8,128)}) custom-call(bf16[5,128,128]{2,1,0:T(8,128)(2,1)} %q_ref.1, bf16[1024,128]{1,0:T(8,128)(2,1)} %k_ref.1, s32[64]{0:T(128)} %doc_ref.1, ...), custom_call_target="tpu_custom_call" | custom-call | tf_op jit(solution)/shard_map/pallas_call | solution.py:368
  29.1 4.0 %shard_map.77 = (f32[5,2,64]{2,1,0:T(2,128)}, f32[5,128,128]{2,1,0:T(8,128)}, f32[384,128]{1,0:T(8,128)}) custom-call(f32[5,2,64]{2,1,0:T(2,128)} %get-tuple-element.9.map_ref, f32[5,64,128]{2,1,0:T(8,128)} %get-tuple-element.10.qp_ref, f32[5,64,128]{2,1,0:T(8,128)} %get-tuple-element.11.qg_ref, f32[128,128]{1,0:T(8,128)} %get-tuple-element.12.both_ref, ...), custom_call_target="tpu_custom_call" | custom-call | tf_op jit(solution)/shard_map/pallas_call | solution.py:396
